TPU v7x, 256 devices: a whole 4x4x8 slice. The times are simulated.
256 devices in a mesh: req: 64 (over z, y, core), head: 4 (over x).
Axes of the slice: x: 4, y: 4, z: 8, core: 2. Of those that a mesh axis runs over, the one named last changes fastest.
Arguments:
- residual: bfloat16 [1024, 2048], P('req'), may hold values from -5.2 to 5.2
- queries: bfloat16 [1024, 1024], P('req', 'head'), may hold values from -5.5 to 5.5
- new_kv: bfloat16 [1024, 2, 1024], P('req', None, 'head'), may hold values from -4.5 to 4.5
- kv_cache: bfloat16 [8192, 2, 32, 1024], P('req', None, None, 'head'), may hold values from -131 to 131
- lengths: int32 [1024], replicated, may hold values from 2 to 16384, as said below
- slot_request: int32 [8192], P('req'), may hold values from 0 to 1023, as said below
- slot_page: int32 [8192], P('req'), may hold values from 0 to 511, as said below
- slot_used: int32 [8192], P('req'), may hold values from 0 to 1
- out_weight: bfloat16 [1024, 2048], P('head'), may hold values from -0.1875 to 0.1875
- norm_gain: float32 [2048], replicated, may hold values from 0.25 to 1.75
- routes: int32 [1024, 8], P('req'), may hold values from 0 to 63, all different within a row; in each aligned block of 16 rows (0 to 15, 16 to 31, ...) at most 4 rows name the same one
- route_weights: float32 [1024, 8], P('req'), may hold values from 0.05 to 0.5
- w_gate: bfloat16 [64, 2048, 1024], P('req', None, 'head'), may hold values from -0.125 to 0.125
- w_up: bfloat16 [64, 2048, 1024], P('req', None, 'head'), may hold values from -0.125 to 0.125
- w_down: bfloat16 [64, 1024, 2048], P('req', 'head'), may hold values from -0.1875 to 0.1875
- next_gain: float32 [2048], replicated, may hold values from 0.25 to 1.75
- next_weight: bfloat16 [2048, 3, 1024], P(None, None, 'head'), may hold values from -0.125 to 0.125
Outputs:
- stream: bfloat16 [1024, 2048], P('req', 'head')
- next_qkv: bfloat16 [1024, 3, 1024], P('req', None, 'head')
Inputs may be any that keep to these rules, and one draw needn't show every extreme that they name: Request r has cached positions 0 to lengths[r] - 1, held in pages 0 to ceil(lengths[r] / 32) - 1; some request is 16384 long. `slot_request`: each page of every request lies in exactly one slot with slot_used 1; unused slots hold request 0. `slot_page`: unused slots hold page 0. `routes`: within the rows of one index of req at most 4 rows name the same expert.
All inputs are finite; a program needn't handle non-finite values.
Results may differ from a plain program's by a relative error of at most 0.025.
Values may be sent and summed in bfloat16 or wider, within the bound.
No kernel may reach another device: no remote copies, remote signals or barrier semaphores. Data moves between devices by JAX's collectives and lax.ppermute only.
A program may use at most 64 MiB of HBM per device.

v0:
```python
import math
import jax
import jax.numpy as jnp
from jax import lax
from jax.sharding import PartitionSpec as P

HD = 128
EXP_DEV = 1
norm_eps = 1e-06
floor_value = -1e30


def norm_whole(rows_in, gain):
    wide_rows = rows_in.astype(jnp.float32)
    mean_square = jnp.mean(wide_rows * wide_rows, axis=1, keepdims=True)
    return (wide_rows * lax.rsqrt(mean_square + norm_eps) * gain).astype(jnp.bfloat16)


def route_tables(routes, route_weights, expert_total, capacity):
    row_count, pick_count = routes.shape
    flat_routes = routes.reshape(row_count * pick_count)
    hit_table = (flat_routes[:, None] == jnp.arange(expert_total, dtype=jnp.int32)[None, :]).astype(
        jnp.int32
    )
    before = jnp.cumsum(hit_table, axis=0) - hit_table
    slot_rank = jnp.sum(before * hit_table, axis=1)
    target = flat_routes * capacity + slot_rank
    lookup = (
        target[:, None] == jnp.arange(expert_total * capacity, dtype=jnp.int32)[None, :]
    ).astype(jnp.float32)
    lookup = lookup.reshape(row_count, pick_count, expert_total * capacity)
    pick_map = jnp.sum(lookup, axis=1)
    blend_map = jnp.sum(lookup * route_weights[:, :, None], axis=1)
    return (pick_map, blend_map)


def expert_block(arrived, w_gate, w_up, w_down):
    gate_out = jnp.einsum("secd,edf->secf", arrived, w_gate, preferred_element_type=jnp.float32)
    upward = jnp.einsum("secd,edf->secf", arrived, w_up, preferred_element_type=jnp.float32)
    inner_act = (jax.nn.silu(gate_out) * upward).astype(jnp.bfloat16)
    return jnp.einsum("secf,efd->secd", inner_act, w_down, preferred_element_type=jnp.float32)


def local(
    residual,
    queries,
    new_kv,
    kv_cache,
    lengths,
    slot_request,
    slot_page,
    slot_used,
    out_weight,
    norm_gain,
    routes,
    route_weights,
    w_gate,
    w_up,
    w_down,
    next_gain,
    next_weight,
):
    req_rows, row_width = queries.shape
    head_count = row_width // HD
    slot_count = kv_cache.shape[0]
    page_len = kv_cache.shape[2]
    model_width = residual.shape[1]
    req_count = lax.axis_size("req")
    head_total = lax.axis_size("head")
    score_scale = 1.0 / math.sqrt(HD)
    first_row = lax.axis_index("req") * req_rows
    everyone = lax.all_gather(queries, "req", axis=0, tiled=True)
    total_req = everyone.shape[0]
    chosen = everyone[slot_request].reshape(slot_count, head_count, HD)
    key_rows = kv_cache[:, 0].reshape(slot_count, page_len, head_count, HD)
    value_rows = kv_cache[:, 1].reshape(slot_count, page_len, head_count, HD)
    scores = (
        jnp.einsum("sphd,shd->sph", key_rows, chosen, preferred_element_type=jnp.float32)
        * score_scale
    )
    position = slot_page[:, None] * page_len + jnp.arange(page_len, dtype=jnp.int32)[None, :]
    valid = (slot_used[:, None] == 1) & (position < lengths[slot_request][:, None])
    masked = jnp.where(valid[:, :, None], scores, floor_value)
    slot_peak = jnp.max(masked, axis=1)
    member = slot_request[None, :] == jnp.arange(total_req, dtype=jnp.int32)[:, None]
    local_peak = jnp.max(jnp.where(member[:, :, None], slot_peak[None], floor_value), axis=1)
    fresh_key = new_kv[:, 0].reshape(req_rows, head_count, HD)
    fresh_value = new_kv[:, 1].astype(jnp.float32).reshape(req_rows, head_count, HD)
    own_query = queries.reshape(req_rows, head_count, HD)
    own_score = (
        jnp.einsum("rhd,rhd->rh", own_query, fresh_key, preferred_element_type=jnp.float32)
        * score_scale
    )
    placed_score = lax.dynamic_update_slice(
        jnp.full((total_req, head_count), floor_value, jnp.float32), own_score, (first_row, 0)
    )
    peak_score = lax.pmax(jnp.maximum(local_peak, placed_score), "req")
    weights = jnp.where(
        valid[:, :, None], jnp.exp(masked - peak_score[slot_request][:, None, :]), 0.0
    ).astype(jnp.bfloat16)
    slot_numer = jnp.einsum(
        "sph,sphd->shd", weights, value_rows, preferred_element_type=jnp.float32
    ).reshape(slot_count, row_width)
    slot_denom = jnp.sum(weights.astype(jnp.float32), axis=1)
    member_float = member.astype(jnp.float32)
    numerator = jnp.dot(member_float, slot_numer, precision=lax.Precision.HIGHEST)
    denominator = jnp.dot(member_float, slot_denom, precision=lax.Precision.HIGHEST)
    numerator, denominator = (
        lax.psum_scatter(numerator, "req", scatter_dimension=0, tiled=True),
        lax.psum_scatter(denominator, "req", scatter_dimension=0, tiled=True),
    )
    own_peak = lax.dynamic_slice_in_dim(peak_score, first_row, req_rows, 0)
    new_lift = jnp.exp(own_score - own_peak)
    mixed_rows = (
        numerator.reshape(req_rows, head_count, HD) + new_lift[:, :, None] * fresh_value
    ) / (denominator + new_lift)[:, :, None]
    attended = mixed_rows.reshape(req_rows, row_width).astype(jnp.bfloat16)
    partial_out = jnp.dot(attended, out_weight, preferred_element_type=jnp.float32)
    expert_total = EXP_DEV * req_count
    pick_count = routes.shape[1]
    capacity = min(
        req_rows, max(2, 2 * ((req_rows * pick_count + expert_total - 1) // expert_total))
    )
    slot_cells = expert_total * capacity
    pick_map, blend_map = route_tables(routes, route_weights, expert_total, capacity)
    pick_bf = pick_map.astype(jnp.bfloat16)
    slice_width = model_width // head_total
    first_col = lax.axis_index("head") * slice_width
    attn_out = lax.psum(partial_out.astype(jnp.bfloat16), "head").astype(jnp.float32)
    hidden_state = (residual.astype(jnp.float32) + attn_out).astype(jnp.bfloat16)
    normed = norm_whole(hidden_state, norm_gain)
    buffer = jnp.einsum("rc,rd->cd", pick_bf, normed, preferred_element_type=jnp.float32).astype(
        jnp.bfloat16
    )
    buffer = buffer.reshape(req_count, EXP_DEV, capacity, model_width)
    expert_part = expert_block(
        lax.all_to_all(buffer, "req", split_axis=0, concat_axis=0, tiled=True), w_gate, w_up, w_down
    )
    expert_sum = lax.psum(expert_part.astype(jnp.bfloat16), "head")
    returned = lax.all_to_all(expert_sum, "req", split_axis=0, concat_axis=0, tiled=True)
    moe_sum = jnp.dot(
        blend_map,
        returned.reshape(slot_cells, model_width).astype(jnp.float32),
        precision=lax.Precision.HIGHEST,
    )
    stream_full = (hidden_state.astype(jnp.float32) + moe_sum).astype(jnp.bfloat16)
    next_normed = norm_whole(stream_full, next_gain)
    stream_out = lax.dynamic_slice_in_dim(stream_full, first_col, slice_width, 1)
    next_qkv = jnp.einsum(
        "td,dcf->tcf", next_normed, next_weight, preferred_element_type=jnp.float32
    ).astype(jnp.bfloat16)
    return (stream_out, next_qkv)


def solution(mesh):
    placed = (
        P("req", None),
        P("req", "head"),
        P("req", None, "head"),
        P("req", None, None, "head"),
        P(),
        P("req"),
        P("req"),
        P("req"),
        P("head", None),
        P(),
        P("req", None),
        P("req", None),
        P("req", None, "head"),
        P("req", None, "head"),
        P("req", "head", None),
        P(),
        P(None, None, "head"),
    )
    return jax.shard_map(
        local,
        mesh=mesh,
        in_specs=placed,
        out_specs=(P("req", "head"), P("req", None, "head")),
        check_vma=False,
    )
```

profile of v0, /device:TPU:1, one launch (start us, length us, event | category | flops | bytes accessed | tf_op | source)
XLA Modules:
  0.0 685.3 jit_solution(6370104238343383896)
XLA Ops:
  8.9 59.8 %all_gather.3 = bf16[1024,256]{1,0:T(8,128)(2,1)} all-gather(bf16[16,256]{1,0:T(8,128)(2,1)} %param.18), channel_id=1, replica_groups=mesh['req'=64,'head'=4] {'req'}, dimensions={0}, use_global_device_ids=true | all-gather | bytes 532480 | tf_op jit(solution)/shard_map/all_gather | solution.py:72
  69.4 1.9 gather_fusion.1
  71.9 4.6 fusion.59
  76.5 4.0 reshape_squeeze.9
  80.5 2.9 fusion.4
  86.2 1.9 max.5
  88.1 247.3 %pmax.7 = f32[1024,2]{1,0:T(8,128)} all-reduce(f32[1024,2]{1,0:T(8,128)} %max.5), channel_id=1, replica_groups=mesh['req'=64,'head'=4] {'req'}, use_global_device_ids=true, to_apply=%region_2.3 | all-reduce | flops 2048 | bytes 16384 | tf_op jit(solution)/shard_map/pmax | solution.py:97
  335.4 1.7 gather_fusion.2
  337.3 4.0 reshape_squeeze.11
  341.3 2.3 fusion.2
  343.6 1.6 fusion.21
  347.7 131.2 %all-reduce = f32[1024,2]{0,1:T(2,128)S(1)} all-reduce(f32[1024,2]{0,1:T(2,128)S(1)} %fusion.20), channel_id=3, replica_groups=mesh['req'=64,'head'=4] {'req'}, use_global_device_ids=true, to_apply=%region_5.6.clone | all-reduce | flops 2048 | bytes 16384
  481.3 2.1 convolution_convert_fusion.2
  483.7 47.1 %all-reduce.4.cloned.1.call-done = bf16[16,2048]{1,0:T(8,128)(2,1)} async-done(((bf16[16,2048]{1,0:T(8,128)(2,1)}), bf16[16,2048]{1,0:T(8,128)(2,1)}) %all-reduce.4.cloned.1.call-update) | async-done | bytes 65552 | tf_op jit(solution)/shard_map/psum | solution.py:129
  531.8 2.3 convolution_convert_fusion.1
  534.1 2.3 reshape.165
  536.3 40.8 %all_to_all.10 = bf16[64,1,4,2048]{3,2,1,0:T(4,128)(2,1)S(1)} all-to-all(bf16[64,1,4,2048]{3,2,1,0:T(4,128)(2,1)} %bitcast.123), channel_id=1, replica_groups=mesh['req'=64,'head'=4] {'req'}, dimensions={0} | all-to-all | bytes 2097152 | tf_op jit(solution)/shard_map/all_to_all | solution.py:137
  579.4 4.2 fusion
  583.7 45.9 %all-reduce.6.cloned.1.call-done = bf16[64,1,4,2048]{3,0,2,1:T(8,128)(2,1)} async-done(((bf16[64,1,4,2048]{3,0,2,1:T(8,128)(2,1)}), bf16[64,1,4,2048]{3,0,2,1:T(8,128)(2,1)}) %all-reduce.6.cloned.1.call-update) | async-done | bytes 1048592 | tf_op jit(solution)/shard_map/psum | solution.py:139
  629.5 3.1 copy.52
  632.6 12.4 %all-to-all-start.1 = ((bf16[64,1,4,2048]{3,2,1,0:T(4,128)(2,1)}), bf16[64,1,4,2048]{3,2,1,0:T(4,128)(2,1)}, u32[]{:S(2)}, u32[]{:S(2)}) async-start(bf16[64,1,4,2048]{3,2,1,0:T(4,128)(2,1)} %copy.52), calls=%async_computation.2 | async-start | bytes 2097152 | tf_op jit(solution)/shard_map/all_to_all | solution.py:140
  645.0 27.9 %all-to-all-done.1 = bf16[64,1,4,2048]{3,2,1,0:T(4,128)(2,1)} async-done(((bf16[64,1,4,2048]{3,2,1,0:T(4,128)(2,1)}), bf16[64,1,4,2048]{3,2,1,0:T(4,128)(2,1)}, u32[]{:S(2)}, u32[]{:S(2)}) %all-to-all-start.1) | async-done | bytes 1048608 | tf_op jit(solution)/shard_map/all_to_all | solution.py:140
  672.9 2.2 reshape.171
  675.1 1.9 fusion.29
  (80 shorter events, 15.5 us)
Async XLA Ops:
  7.2 670.4 %copy-start = (bf16[2048,3,256]{2,0,1:T(8,128)(2,1)S(1)}, bf16[2048,3,256]{2,0,1:T(8,128)(2,1)}, u32[]{:S(2)}) copy-start(bf16[2048,3,256]{2,0,1:T(8,128)(2,1)} %param.33) | copy-start | bytes 9437188
  7.2 474.0 %reduce-scatter.3.cloned.1.call-start = ((), (), s32[]{:S(2)}) async-start(), calls=%async_computation.3 | async-start | bytes 1064960 | tf_op jit(solution)/shard_map/reduce_scatter | solution.py:109
  80.5 3.0 copy-start.1
  80.5 4.0 copy-start.12
  80.5 4.0 copy-start.13
  80.5 5.5 copy-start.5
  341.3 2.3 copy-start.10
  341.3 4.0 copy-start.8
  341.3 4.7 copy-start.9
  341.3 4.8 copy-start.14
  343.6 187.2 %copy-start.3 = (bf16[16,2048]{1,0:T(8,128)(2,1)S(1)}, bf16[16,2048]{1,0:T(8,128)(2,1)}, u32[]{:S(2)}) copy-start(bf16[16,2048]{1,0:T(8,128)(2,1)} %param.17) | copy-start | bytes 196612
  343.6 188.1 %copy-start.6 = (f32[2048]{0:T(1024)S(1)}, f32[2048]{0:T(1024)}, u32[]{:S(2)}) copy-start(f32[2048]{0:T(1024)} %param.26) | copy-start | bytes 24580
  345.2 185.5 %all-reduce.4.cloned.1.call-start = ((), (), s32[]{:S(2)}) async-start(), calls=%async_computation.4 | async-start | bytes 131072 | tf_op jit(solution)/shard_map/psum | solution.py:129
  483.5 146.1 %all-reduce.6.cloned.1.call-start = ((), (), s32[]{:S(2)}) async-start(), calls=%async_computation.5 | async-start | bytes 2097152 | tf_op jit(solution)/shard_map/psum | solution.py:139
  536.3 41.8 %copy-start.11 = (bf16[1,2048,256]{2,1,0:T(8,128)(2,1)S(1)}, bf16[1,2048,256]{2,1,0:T(8,128)(2,1)}, u32[]{:S(2)}) copy-start(bf16[1,2048,256]{2,1,0:T(8,128)(2,1)} %param.29) | copy-start | bytes 3145732
  577.2 1.0 copy-start.2
  632.6 42.5 %copy-start.4 = (bf16[16,2048]{1,0:T(8,128)(2,1)S(1)}, bf16[16,2048]{1,0:T(8,128)(2,1)}, u32[]{:S(2)}) copy-start(bf16[16,2048]{1,0:T(8,128)(2,1)} %all-reduce.4.cloned.1.call-done) | copy-start | bytes 196612
  632.6 40.3 %all-to-all-start.1 = ((bf16[64,1,4,2048]{3,2,1,0:T(4,128)(2,1)}), bf16[64,1,4,2048]{3,2,1,0:T(4,128)(2,1)}, u32[]{:S(2)}, u32[]{:S(2)}) async-start(bf16[64,1,4,2048]{3,2,1,0:T(4,128)(2,1)} %copy.52), calls=%async_computation.2 | async-start | bytes 2097152 | tf_op jit(solution)/shard_map/all_to_all | solution.py:140
  645.0 32.6 %copy-start.7 = (f32[2048]{0:T(1024)S(1)}, f32[2048]{0:T(1024)}, u32[]{:S(2)}) copy-start(f32[2048]{0:T(1024)} %param.32) | copy-start | bytes 24580
Sparse Core Ops, SparseCore 0:
  345.4 135.7 reduce-scatter.2
  483.6 47.1 all-reduce.3
  583.8 45.6 all-reduce.5
where the time goes:
time: 686 us; the launch traced here: 685 us
  blocking collectives  479 us (70%)
  waiting for transfers between devices  122 us (18%)
  local copies, waits for them, and re-layouts  30.3 us (4%)
  matrix products  20 us (3%)
  between operations  14.6 us (2%)
  starting transfers between devices  12.5 us (2%)
    pmax x1, blocking collectives, local(): peak_score = lax.pmax(jnp.maximum(local_peak, placed_score), 'req')  247 us
    unnamed x1, blocking collectives  131 us
    all_gather x1, blocking collectives, local(): everyone = lax.all_gather(queries, 'req', axis=0, tiled=True)  59.8 us
    psum x1, waiting for transfers between devices, local(): lax.psum(partial_out.astype(jnp.bfloat16), 'head').astype(jnp.float32)  47.1 us
    psum x1, waiting for transfers between devices, local(): expert_sum = lax.psum(expert_part.astype(jnp.bfloat16), 'head')  45.9 us
    all_to_all x1, blocking collectives, local(): lax.all_to_all(buffer, 'req', split_axis=0, concat_axis=0, tiled=True)  40.8 us
    all_to_all x1, waiting for transfers between devices, local(): lax.all_to_all(expert_sum, 'req', split_axis=0, concat_axis=0, tiled=True)  27.9 us
  transfers between devices with their start and end apart: 4, of which 4 were waited for; matrix products, arithmetic and copies ran while one was open for 0% of the time, Pallas kernels for 0%

commit v1 on v0

--- a/solution.py
+++ b/solution.py
@@ -8,6 +8,11 @@
 EXP_DEV = 1
 norm_eps = 1e-06
 floor_value = -1e30
+
+
+def swapped_in(x, name, dim):
+    stack = jnp.stack([x] * lax.axis_size(name))
+    return jnp.concatenate(lax.all_to_all(stack, name, 0, 0), axis=dim)
 
 
 def norm_whole(rows_in, gain):
@@ -69,7 +74,7 @@
     head_total = lax.axis_size("head")
     score_scale = 1.0 / math.sqrt(HD)
     first_row = lax.axis_index("req") * req_rows
-    everyone = lax.all_gather(queries, "req", axis=0, tiled=True)
+    everyone = swapped_in(queries, "req", 0)
     total_req = everyone.shape[0]
     chosen = everyone[slot_request].reshape(slot_count, head_count, HD)
     key_rows = kv_cache[:, 0].reshape(slot_count, page_len, head_count, HD)

time: 686 us -> 644 us (0.939)
  blocking collectives: 479 us -> 420 us
  starting transfers between devices: 12.5 us -> 25.9 us
    all_gather x1 -> x0, blocking collectives: 59.8 us -> none  [local(): everyone = lax.all_gather(queries, 'req', axis=0, tiled=True)]
    all_to_all x0 -> x1, starting transfers between devices: none -> 13.3 us  [swapped_in(): return jnp.concatenate(lax.all_to_all(stack, name, 0, 0), axis=dim)]
  transfers between devices with their start and end apart: 4 -> 5, of which waited for: 4 -> 5; matrix products, arithmetic and copies ran while one was open for 0% -> 3% of each run, Pallas kernels for 0% -> 0%
where the time goes in v1:
time: 644 us; the launch traced here: 643 us
  blocking collectives  420 us (65%)
  waiting for transfers between devices  124 us (19%)
  local copies, waits for them, and re-layouts  32.2 us (5%)
  starting transfers between devices  25.9 us (4%)
  matrix products  19.9 us (3%)
  between operations  14.7 us (2%)
    pmax x1, blocking collectives, local(): peak_score = lax.pmax(jnp.maximum(local_peak, placed_score), 'req')  248 us
    unnamed x1, blocking collectives  131 us
    psum x1, waiting for transfers between devices, local(): lax.psum(partial_out.astype(jnp.bfloat16), 'head').astype(jnp.float32)  47.1 us
    psum x1, waiting for transfers between devices, local(): expert_sum = lax.psum(expert_part.astype(jnp.bfloat16), 'head')  45.9 us
    all_to_all x1, blocking collectives, local(): lax.all_to_all(buffer, 'req', split_axis=0, concat_axis=0, tiled=True)  40.8 us
    all_to_all x1, waiting for transfers between devices, local(): lax.all_to_all(expert_sum, 'req', split_axis=0, concat_axis=0, tiled=True)  27.9 us
    all_to_all x1, starting transfers between devices, swapped_in(): return jnp.concatenate(lax.all_to_all(stack, name, 0, 0), axis=dim)  13.3 us
  transfers between devices with their start and end apart: 5, of which 5 were waited for; matrix products, arithmetic and copies ran while one was open for 3% of the time, Pallas kernels for 0%

profile of v1, /device:TPU:1, one launch (start us, length us, event | category | flops | bytes accessed | tf_op | source)
XLA Modules:
  0.0 643.1 jit_solution(2674278678109125508)
XLA Ops:
  7.2 1.7 stack.2
  8.9 13.3 %all-to-all-start = ((bf16[64,16,256]{2,1,0:T(8,128)(2,1)}), bf16[64,16,256]{2,1,0:T(8,128)(2,1)}, u32[]{:S(2)}, u32[]{:S(2)}) async-start(bf16[64,16,256]{2,1,0:T(8,128)(2,1)} %stack.2), calls=%async_computation | async-start | bytes 1048576 | tf_op jit(solution)/shard_map/all_to_all | solution.py:15
  23.0 4.7 fusion.59
  27.8 4.0 reshape_squeeze.9
  31.8 4.0 reshape_squeeze.11
  39.9 1.9 gather_fusion.1
  42.4 2.8 fusion.4
  46.8 2.1 max.5
  48.8 248.4 %pmax.7 = f32[1024,2]{1,0:T(8,128)} all-reduce(f32[1024,2]{1,0:T(8,128)} %max.5), channel_id=1, replica_groups=mesh['req'=64,'head'=4] {'req'}, use_global_device_ids=true, to_apply=%region_2.3 | all-reduce | flops 2048 | bytes 16384 | tf_op jit(solution)/shard_map/pmax | solution.py:102
  297.2 1.7 gather_fusion.2
  299.2 2.2 fusion.2
  305.5 131.3 %all-reduce = f32[1024,2]{0,1:T(2,128)S(1)} all-reduce(f32[1024,2]{0,1:T(2,128)S(1)} %fusion.20), channel_id=3, replica_groups=mesh['req'=64,'head'=4] {'req'}, use_global_device_ids=true, to_apply=%region_5.6.clone | all-reduce | flops 2048 | bytes 16384
  439.1 2.1 convolution_convert_fusion.2
  441.5 47.1 %all-reduce.4.cloned.1.call-done = bf16[16,2048]{1,0:T(8,128)(2,1)} async-done(((bf16[16,2048]{1,0:T(8,128)(2,1)}), bf16[16,2048]{1,0:T(8,128)(2,1)}) %all-reduce.4.cloned.1.call-update) | async-done | bytes 65552 | tf_op jit(solution)/shard_map/psum | solution.py:134
  489.5 2.3 convolution_convert_fusion.1
  491.8 2.3 reshape.171
  494.1 40.8 %all_to_all.15 = bf16[64,1,4,2048]{3,2,1,0:T(4,128)(2,1)S(1)} all-to-all(bf16[64,1,4,2048]{3,2,1,0:T(4,128)(2,1)} %bitcast.124), channel_id=1, replica_groups=mesh['req'=64,'head'=4] {'req'}, dimensions={0} | all-to-all | bytes 2097152 | tf_op jit(solution)/shard_map/all_to_all | solution.py:142
  537.2 4.2 fusion
  541.4 45.9 %all-reduce.6.cloned.1.call-done = bf16[64,1,4,2048]{3,0,2,1:T(8,128)(2,1)} async-done(((bf16[64,1,4,2048]{3,0,2,1:T(8,128)(2,1)}), bf16[64,1,4,2048]{3,0,2,1:T(8,128)(2,1)}) %all-reduce.6.cloned.1.call-update) | async-done | bytes 1048592 | tf_op jit(solution)/shard_map/psum | solution.py:144
  587.3 3.1 copy.52
  590.4 12.4 %all-to-all-start.2 = ((bf16[64,1,4,2048]{3,2,1,0:T(4,128)(2,1)}), bf16[64,1,4,2048]{3,2,1,0:T(4,128)(2,1)}, u32[]{:S(2)}, u32[]{:S(2)}) async-start(bf16[64,1,4,2048]{3,2,1,0:T(4,128)(2,1)} %copy.52), calls=%async_computation.3 | async-start | bytes 2097152 | tf_op jit(solution)/shard_map/all_to_all | solution.py:145
  602.8 27.9 %all-to-all-done.2 = bf16[64,1,4,2048]{3,2,1,0:T(4,128)(2,1)} async-done(((bf16[64,1,4,2048]{3,2,1,0:T(4,128)(2,1)}), bf16[64,1,4,2048]{3,2,1,0:T(4,128)(2,1)}, u32[]{:S(2)}, u32[]{:S(2)}) %all-to-all-start.2) | async-done | bytes 1048608 | tf_op jit(solution)/shard_map/all_to_all | solution.py:145
  630.7 2.2 reshape.177
  632.9 1.9 fusion.29
  (84 shorter events, 18.2 us)
Async XLA Ops:
  7.2 628.2 %copy-start = (bf16[2048,3,256]{2,0,1:T(8,128)(2,1)S(1)}, bf16[2048,3,256]{2,0,1:T(8,128)(2,1)}, u32[]{:S(2)}) copy-start(bf16[2048,3,256]{2,0,1:T(8,128)(2,1)} %param.33) | copy-start | bytes 9437188
  8.9 31.0 %all-to-all-start = ((bf16[64,16,256]{2,1,0:T(8,128)(2,1)}), bf16[64,16,256]{2,1,0:T(8,128)(2,1)}, u32[]{:S(2)}, u32[]{:S(2)}) async-start(bf16[64,16,256]{2,1,0:T(8,128)(2,1)} %stack.2), calls=%async_computation | async-start | bytes 1048576 | tf_op jit(solution)/shard_map/all_to_all | solution.py:15
  22.2 416.7 %reduce-scatter.3.cloned.1.call-start = ((), (), s32[]{:S(2)}) async-start(), calls=%async_computation.4 | async-start | bytes 1064960 | tf_op jit(solution)/shard_map/reduce_scatter | solution.py:114
  22.9 4.7 copy-start.13
  22.9 4.7 copy-start.5
  22.9 4.8 copy-start.6
  31.8 4.0 copy-start.1
  31.8 5.1 copy-start.14
  31.8 6.5 %copy-start.11 = (s32[128]{0:T(128)S(1)}, s32[128]{0:T(128)}, u32[]{:S(2)}) copy-start(s32[128]{0:T(128)} %param.22) | copy-start | bytes 1540
  299.2 4.0 copy-start.9
  299.2 4.7 copy-start.10
  299.2 4.7 copy-start.15
  301.4 187.1 %copy-start.3 = (bf16[16,2048]{1,0:T(8,128)(2,1)S(1)}, bf16[16,2048]{1,0:T(8,128)(2,1)}, u32[]{:S(2)}) copy-start(bf16[16,2048]{1,0:T(8,128)(2,1)} %param.17) | copy-start | bytes 196612
  301.5 188.1 %copy-start.7 = (f32[2048]{0:T(1024)S(1)}, f32[2048]{0:T(1024)}, u32[]{:S(2)}) copy-start(f32[2048]{0:T(1024)} %param.26) | copy-start | bytes 24580
  303.1 185.5 %all-reduce.4.cloned.1.call-start = ((), (), s32[]{:S(2)}) async-start(), calls=%async_computation.5 | async-start | bytes 131072 | tf_op jit(solution)/shard_map/psum | solution.py:134
  441.3 146.0 %all-reduce.6.cloned.1.call-start = ((), (), s32[]{:S(2)}) async-start(), calls=%async_computation.6 | async-start | bytes 2097152 | tf_op jit(solution)/shard_map/psum | solution.py:144
  494.1 41.8 %copy-start.12 = (bf16[1,2048,256]{2,1,0:T(8,128)(2,1)S(1)}, bf16[1,2048,256]{2,1,0:T(8,128)(2,1)}, u32[]{:S(2)}) copy-start(bf16[1,2048,256]{2,1,0:T(8,128)(2,1)} %param.29) | copy-start | bytes 3145732
  534.9 1.0 copy-start.2
  590.4 42.5 %copy-start.4 = (bf16[16,2048]{1,0:T(8,128)(2,1)S(1)}, bf16[16,2048]{1,0:T(8,128)(2,1)}, u32[]{:S(2)}) copy-start(bf16[16,2048]{1,0:T(8,128)(2,1)} %all-reduce.4.cloned.1.call-done) | copy-start | bytes 196612
  590.4 40.3 %all-to-all-start.2 = ((bf16[64,1,4,2048]{3,2,1,0:T(4,128)(2,1)}), bf16[64,1,4,2048]{3,2,1,0:T(4,128)(2,1)}, u32[]{:S(2)}, u32[]{:S(2)}) async-start(bf16[64,1,4,2048]{3,2,1,0:T(4,128)(2,1)} %copy.52), calls=%async_computation.3 | async-start | bytes 2097152 | tf_op jit(solution)/shard_map/all_to_all | solution.py:145
  602.8 32.6 %copy-start.8 = (f32[2048]{0:T(1024)S(1)}, f32[2048]{0:T(1024)}, u32[]{:S(2)}) copy-start(f32[2048]{0:T(1024)} %param.32) | copy-start | bytes 24580
Sparse Core Ops, SparseCore 0:
  303.2 135.7 reduce-scatter.2
  441.4 47.1 all-reduce.3
  541.6 45.7 all-reduce.5
